TPU v7x, 32 devices: a whole 2x2x4 slice. The times are simulated.
32 devices in a mesh: groups: 2 (over y), pts: 16 (over z, x, core).
Axes of the slice: x: 2, y: 2, z: 4, core: 2. Of those that a mesh axis runs over, the one named last changes fastest.
Arguments:
- latents: bfloat16 [2048, 768], P(('groups', 'pts')), parts along dimension 0, may hold values from -160 to 160
- points: bfloat16 [12288, 768], P(('groups', 'pts')), parts along dimension 0, may hold values from -6 to 6
- counts: int32 [32], P(('groups', 'pts')), parts along dimension 0, may hold values from 48 to 384, as said below
- w_query: bfloat16 [768, 768], replicated, may hold values from -0.21875 to 0.21875
- w_key: bfloat16 [768, 768], replicated, may hold values from -0.21875 to 0.21875
- w_value: bfloat16 [768, 768], replicated, may hold values from -0.21875 to 0.21875
- w_out: bfloat16 [768, 768], replicated, may hold values from -0.21875 to 0.21875
- d_out: bfloat16 [2048, 768], P(('groups', 'pts')), parts along dimension 0, may hold values from -6 to 6
Outputs:
- result: bfloat16 [2048, 768], P(('groups', 'pts')), parts along dimension 0
- d_latents: bfloat16 [2048, 768], P(('groups', 'pts')), parts along dimension 0
- d_points: bfloat16 [12288, 768], P(('groups', 'pts')), parts along dimension 0
There are 2 independent parts, one for each index of `groups`. A program takes and returns all parts, laid end to end along the dimension named above; an argument that names none is the same for every part. Nothing has to cross between parts.
Inputs may be any that keep to these rules, and one draw needn't show every extreme that they name: counts[s] live points fill the first slots of block s; in every part one block is full with 384 and another holds only 48.
All inputs are finite; a program needn't handle non-finite values.
Results may differ from a plain program's by a relative error of at most 0.018.
The roundings to bfloat16 on the way count: a program that leaves them out, or rounds other values in their place, can miss the bound.
Values may be sent and summed in bfloat16 or wider, within the bound.
No kernel may reach another device: no remote copies, remote signals or barrier semaphores. Data moves between devices by JAX's collectives and lax.ppermute only.
A program may use at most 128 MiB of HBM per device.

v0:
```python
import jax
import jax.numpy as jnp
from jax import lax
from jax.sharding import PartitionSpec as P

HEADS = 12


def masked_scores(query_head, key_head, live_mask):
    raw = jnp.dot(query_head, key_head.T, preferred_element_type=jnp.float32) * 0.125
    return jnp.where(live_mask[None, :], raw, -jnp.inf)


def body(latents, points, counts, w_query, w_key, w_value, w_out, d_out):
    own_rows, width = latents.shape
    slots = points.shape[0]
    head_dim = width // HEADS
    key_rows = jnp.dot(points, w_key, preferred_element_type=jnp.float32).astype(jnp.bfloat16)
    value_rows = jnp.dot(points, w_value, preferred_element_type=jnp.float32).astype(jnp.bfloat16)
    live_mask = jnp.arange(slots, dtype=jnp.int32) < counts[0]
    query_own = jnp.dot(latents, w_query, preferred_element_type=jnp.float32).astype(jnp.bfloat16)
    query_all = lax.all_gather(query_own, "pts", axis=0, tiled=True)
    query_count = query_all.shape[0]

    def split_heads(matrix):
        return matrix.reshape(matrix.shape[0], HEADS, head_dim).transpose(1, 0, 2)

    def join_heads(stack):
        return stack.transpose(1, 0, 2).reshape(stack.shape[1], width)

    query_heads = split_heads(query_all)
    key_heads = split_heads(key_rows)
    value_heads = split_heads(value_rows)

    def local_max(operands):
        query_head, key_head = operands
        return jnp.max(masked_scores(query_head, key_head, live_mask), axis=1)

    row_max = lax.pmax(lax.map(local_max, (query_heads, key_heads)), "pts")

    def partial_attend(operands):
        query_head, key_head, value_head, max_head = operands
        weights = jnp.exp(masked_scores(query_head, key_head, live_mask) - max_head[:, None])
        numerator = jnp.dot(
            weights.astype(jnp.bfloat16), value_head, preferred_element_type=jnp.float32
        )
        return (jnp.sum(weights, axis=1), numerator)

    totals, numerators = lax.map(partial_attend, (query_heads, key_heads, value_heads, row_max))
    numerator = join_heads(numerators)
    total_cols = totals.T
    start = lax.axis_index("pts") * own_rows
    grad_attended = jnp.dot(d_out, w_out.T, preferred_element_type=jnp.float32).astype(jnp.bfloat16)
    numer_all, total_all = lax.psum((numerator, total_cols), "pts")
    attended_all = (numer_all / jnp.repeat(total_all, head_dim, axis=1)).astype(jnp.bfloat16)
    attended = lax.dynamic_slice_in_dim(attended_all, start, own_rows, 0)
    result = (
        latents.astype(jnp.float32) + jnp.dot(attended, w_out, preferred_element_type=jnp.float32)
    ).astype(jnp.bfloat16)
    grad_all = lax.all_gather(grad_attended, "pts", axis=0, tiled=True)
    delta_all = jnp.sum(
        (grad_all.astype(jnp.float32) * attended_all.astype(jnp.float32)).reshape(
            query_count, HEADS, head_dim
        ),
        axis=2,
    )
    lse_all = row_max.T + jnp.log(total_all)

    def backward_head(operands):
        query_head, key_head, value_head, grad_head, lse_head, delta_head = operands
        probability = jnp.exp(masked_scores(query_head, key_head, live_mask) - lse_head[:, None])
        grad_value = jnp.dot(
            probability.astype(jnp.bfloat16).T, grad_head, preferred_element_type=jnp.float32
        )
        grad_weights = jnp.dot(grad_head, value_head.T, preferred_element_type=jnp.float32)
        grad_scores = (probability * (grad_weights - delta_head[:, None])).astype(jnp.bfloat16)
        grad_query = jnp.dot(grad_scores, key_head, preferred_element_type=jnp.float32) * 0.125
        grad_key = jnp.dot(grad_scores.T, query_head, preferred_element_type=jnp.float32) * 0.125
        return (grad_query, grad_key, grad_value)

    grad_query, grad_key, grad_value = lax.map(
        backward_head,
        (query_heads, key_heads, value_heads, split_heads(grad_all), lse_all.T, delta_all.T),
    )
    grad_query_own = lax.psum_scatter(
        join_heads(grad_query), "pts", scatter_dimension=0, tiled=True
    )
    d_latents = (
        d_out.astype(jnp.float32)
        + jnp.dot(
            grad_query_own.astype(jnp.bfloat16), w_query.T, preferred_element_type=jnp.float32
        )
    ).astype(jnp.bfloat16)
    d_points = (
        jnp.dot(
            join_heads(grad_key).astype(jnp.bfloat16), w_key.T, preferred_element_type=jnp.float32
        )
        + jnp.dot(
            join_heads(grad_value).astype(jnp.bfloat16),
            w_value.T,
            preferred_element_type=jnp.float32,
        )
    ).astype(jnp.bfloat16)
    return (result, d_latents, d_points)


def solution(mesh):
    in_specs = (
        P(("groups", "pts"), None),
        P(("groups", "pts"), None),
        P(("groups", "pts")),
        P(),
        P(),
        P(),
        P(),
        P(("groups", "pts"), None),
    )
    out_specs = (P(("groups", "pts"), None), P(("groups", "pts"), None), P(("groups", "pts"), None))
    return jax.shard_map(body, mesh=mesh, in_specs=in_specs, out_specs=out_specs, check_vma=False)
```

profile of v0, /device:TPU:0, one launch (start us, length us, event | category | flops | bytes accessed | tf_op | source)
XLA Modules:
  0.0 493.8 jit_solution(4530850203376139020)
XLA Ops:
  7.3 2.4 convolution_convert_fusion.3
  9.8 2.0 convolution_convert_fusion.2
  17.7 35.6 %all-gather.3.cloned.1.call-done = bf16[1024,768]{1,0:T(8,128)(2,1)} async-done(((bf16[64,768]{1,0:T(8,128)(2,1)}), bf16[1024,768]{1,0:T(8,128)(2,1)}) %all-gather.3.cloned.1.call-update) | async-done | bytes 1572880 | tf_op jit(solution)/shard_map/all_gather | solution.py:22
  55.0 2.7 copy.38
  57.8 25.9 %while.39 = (s32[]{:T(128)}, f32[12,1024]{1,0:T(8,128)S(1)}, bf16[12,1024,64]{2,1,0:T(8,128)(2,1)}, bf16[12,384,64]{2,1,0:T(8,128)(2,1)}, s32[]{:T(128)}, /*index=5*/s32[]{:T(128)}, s32[]{:T(128)}) while((s32[]{:T(128)}, f32[12,1024]{1,0:T(8,128)S(1)}, bf16[12,1024,64]{2,1,0:T(8,128)(2,1)}, bf16[12,384,64]{2,1,0:T(8,128)(2,1)}, ...), condition=%wide.region_2.3_spmd.clone, body=%wide.region_0.2_spmd.clone.sunk | while | flops 51510656 | bytes 374621 | solution.py:39
  83.6 59.7 %pmax.7 = f32[12,1024]{1,0:T(8,128)S(1)} all-reduce(f32[12,1024]{1,0:T(8,128)S(1)} %get-tuple-element.132), channel_id=1, replica_groups=mesh['groups'=2,'pts'=16] {'pts'}, use_global_device_ids=true, to_apply=%region_3.4 | all-reduce | flops 12288 | bytes 98304 | tf_op jit(solution)/shard_map/pmax | solution.py:39
  143.3 2.1 broadcast.28.clone
  145.4 50.3 %while.40 = (s32[]{:T(128)}, f32[12,1024]{1,0:T(8,128)S(1)}, f32[12,1024,64]{1,2,0:T(8,128)}, bf16[12,1024,64]{2,1,0:T(8,128)(2,1)}, bf16[12,384,64]{2,1,0:T(8,1...) while((s32[]{:T(128)}, f32[12,1024]{1,0:T(8,128)S(1)}, ...), condition=%wide.region_6.7_spmd.clone, body=%wide.region_4.6_spmd.clone.sunk | while | flops 102628736 | bytes 2321273 | solution.py:49
  195.7 3.6 copy.41
  199.4 58.6 %psum.15 = f32[1024,12]{0,1:T(8,128)S(1)} all-reduce(f32[1024,12]{0,1:T(8,128)S(1)} %bitcast.173), channel_id=1, replica_groups=mesh['groups'=2,'pts'=16] {'pts'}, use_global_device_ids=true, to_apply=%region_8.9 | all-reduce | flops 12288 | bytes 98304 | tf_op jit(solution)/shard_map/psum | solution.py:54
  258.0 2.0 broadcast_in_dim.58
  260.0 3.5 copy.42
  263.6 2.7 copy.43
  266.3 34.2 %all-reduce.2.cloned.1.call-done = f32[1024,768]{1,0:T(8,128)} async-done(((f32[1024,768]{1,0:T(8,128)}), f32[1024,768]{1,0:T(8,128)}) %all-reduce.2.cloned.1.call-update) | async-done | bytes 3145744 | tf_op jit(solution)/shard_map/psum | solution.py:54
  300.5 5.6 %convert_multiply_fusion = (f32[1024,768]{1,0:T(8,128)}, bf16[1024,768]{1,0:T(8,128)(2,1)}) fusion(bf16[1024,768]{1,0:T(8,128)(2,1)S(1)} %copy-done.1, f32[1024,768]{1,0:T(8,128)} %all-reduce.2.cloned.1.call-done, f32[1024,768]{1,0:T(8,128)} %copy.42), kind=kLoop, calls=%fused_computation.57 | loop fusion | flops 3932160 | bytes 12582912 | tf_op jit(solution)/shard_map/mul | solution.py:62
  306.1 3.6 copy.44
  309.7 2.3 reduce_sum.18
  311.9 2.1 broadcast.28
  314.0 102.0 %while.41 = (s32[]{:T(128)}, f32[12,1024,64]{1,2,0:T(8,128)}, bf16[12,384,64]{1,2,0:T(8,128)(2,1)}, bf16[12,384,64]{1,2,0:T(8,128)(2,1)S(1)}, bf16[12,1024,64]{2...) while((s32[]{:T(128)}, f32[12,1024,64]{1,2,0:T(8,128)}, ...), condition=%wide.region_11.12_spmd.clone, body=%wide.region_10.11_spmd.clone.sunk | while | flops 254501248 | bytes 8648581 | solution.py:81
  360.0 2.0 fusion.108
  368.5 2.0 fusion.108
  385.5 2.0 fusion.108
  416.0 3.5 copy.49
  426.1 58.9 %reduce-scatter.4.cloned.1.call-done = f32[64,768]{1,0:T(8,128)} async-done(((f32[1024,768]{1,0:T(8,128)}), f32[64,768]{1,0:T(8,128)}) %reduce-scatter.4.cloned.1.call-update) | async-done | bytes 196624
  (223 shorter events, 187.4 us)
Async XLA Ops:
  7.2 4.7 copy-start
  7.2 2.6 copy-start.3
  7.2 4.7 copy-start.9
  7.2 46.1 %all-gather.3.cloned.1.call-start = ((), (), s32[]{:S(2)}) async-start(), calls=%async_computation.1 | async-start | bytes 1671168 | tf_op jit(solution)/shard_map/all_gather | solution.py:22
  9.7 253.8 %all-gather.5.cloned.1.call-start = ((), (), s32[]{:S(2)}) async-start(), calls=%async_computation.3 | async-start | bytes 1671168 | tf_op jit(solution)/shard_map/all_gather | solution.py:60
  11.8 288.6 %all-reduce.2.cloned.1.call-start = ((), (), s32[]{:S(2)}) async-start(), calls=%async_computation.2 | async-start | bytes 6291456 | tf_op jit(solution)/shard_map/psum | solution.py:54
  12.6 1.8 copy-start.5
  199.3 285.7 %reduce-scatter.4.cloned.1.call-start = ((), (), s32[]{:S(2)}) async-start(), calls=%async_computation.4 | async-start | bytes 3342336
  263.6 36.9 %copy-start.1 = (bf16[1024,768]{1,0:T(8,128)(2,1)S(1)}, bf16[1024,768]{1,0:T(8,128)(2,1)}, u32[]{:S(2)}) copy-start(bf16[1024,768]{1,0:T(8,128)(2,1)} %all-gather.5.cloned.1.call-done) | copy-start | bytes 4718596
  419.6 1.3 copy-start.4
  419.6 1.3 copy-start.8
  422.7 1.8 copy-start.6
  424.6 61.6 %copy-start.2 = (bf16[768,768]{1,0:T(8,128)(2,1)S(1)}, bf16[768,768]{1,0:T(8,128)(2,1)}, u32[]{:S(2)}) copy-start(bf16[768,768]{1,0:T(8,128)(2,1)} %param.17) | copy-start | bytes 3538948
  424.6 61.6 %copy-start.7 = (bf16[64,768]{1,0:T(8,128)(2,1)S(1)}, bf16[64,768]{1,0:T(8,128)(2,1)}, u32[]{:S(2)}) copy-start(bf16[64,768]{1,0:T(8,128)(2,1)} %param.21) | copy-start | bytes 294916
Sparse Core Ops, SparseCore 0:
  10.9 42.3 all-gather.2
  56.1 38.5 all-gather.4
  199.4 101.0 all-reduce.1
  419.7 65.2 reduce-scatter.3
where the time goes:
time: 497 us; the launch traced here: 494 us
  matrix products  164 us (33%)
  waiting for transfers between devices  129 us (26%)
  blocking collectives  118 us (24%)
  local copies, waits for them, and re-layouts  36.3 us (7%)
  other arithmetic  31.3 us (6%)
  between operations  14 us (3%)
    pmax x1, blocking collectives, body(): row_max = lax.pmax(lax.map(local_max, (query_heads, key_heads)), 'pts')  59.7 us
    unnamed x5, waiting for transfers between devices  59 us
    psum x1, blocking collectives, body(): numer_all, total_all = lax.psum((numerator, total_cols), 'pts')  58.6 us
    dot_general x36, matrix products, masked_scores(): jnp.dot(query_head, key_head.T, preferred_element_type=jnp.float32) * 0.125  51.5 us
    all_gather x1, waiting for transfers between devices, body(): query_all = lax.all_gather(query_own, 'pts', axis=0, tiled=True)  35.6 us
    psum x1, waiting for transfers between devices, body(): numer_all, total_all = lax.psum((numerator, total_cols), 'pts')  34.2 us
    dot_general x12, matrix products, backward_head(): jnp.dot(grad_scores, key_head, preferred_element_type=jnp.float32) * 0.125  23.7 us
    lt x36, other arithmetic, body(): live_mask = jnp.arange(slots, dtype=jnp.int32) < counts[0]  23.4 us
  transfers between devices with their start and end apart: 4, of which 3 were waited for; matrix products, arithmetic and copies ran while one was open for 22% of the time, Pallas kernels for 0%

commit v1 on v0

--- a/solution.py
+++ b/solution.py
@@ -4,6 +4,27 @@
 from jax.sharding import PartitionSpec as P
 
 HEADS = 12
+
+
+def laid_out(blocks, dim):
+    shape = list(blocks.shape[1:])
+    shape[dim] *= blocks.shape[0]
+    return jnp.moveaxis(blocks, 0, dim).reshape(shape)
+
+
+def grow_blocks(x, axis):
+    peers, index = (lax.axis_size(axis), lax.axis_index(axis))
+    tiles, stride = (x[None], 1)
+    while stride < peers:
+        theirs = lax.ppermute(tiles, axis, [(i, i ^ stride) for i in range(peers)])
+        low = index & stride == 0
+        tiles = jnp.concatenate([jnp.where(low, tiles, theirs), jnp.where(low, theirs, tiles)])
+        stride *= 2
+    return tiles
+
+
+def gather_by_bits(value, axis, dim):
+    return laid_out(grow_blocks(value, axis), dim)
 
 
 def masked_scores(query_head, key_head, live_mask):
@@ -19,7 +40,7 @@
     value_rows = jnp.dot(points, w_value, preferred_element_type=jnp.float32).astype(jnp.bfloat16)
     live_mask = jnp.arange(slots, dtype=jnp.int32) < counts[0]
     query_own = jnp.dot(latents, w_query, preferred_element_type=jnp.float32).astype(jnp.bfloat16)
-    query_all = lax.all_gather(query_own, "pts", axis=0, tiled=True)
+    query_all = gather_by_bits(query_own, "pts", 0)
     query_count = query_all.shape[0]
 
     def split_heads(matrix):

time: 497 us -> 522 us (1.050)
  local copies, waits for them, and re-layouts: 36.3 us -> 45 us
  starting transfers between devices: 0.16 us -> 8.02 us
    ppermute x0 -> x4, waiting for transfers between devices: none -> 40.6 us  [grow_blocks(): theirs = lax.ppermute(tiles, axis, [(i, i ^ stride) for i in range(peers)])]
    all_gather x1 -> x0, waiting for transfers between devices: 35.6 us -> none  [body(): query_all = lax.all_gather(query_own, 'pts', axis=0, tiled=True)]
    ppermute x0 -> x4, starting transfers between devices: none -> 7.9 us  [grow_blocks(): theirs = lax.ppermute(tiles, axis, [(i, i ^ stride) for i in range(peers)])]
    unnamed x5 -> x4, waiting for transfers between devices: 59 us -> 59 us
    unnamed x25 -> x23, local copies, waits for them, and re-layouts: 11.5 us -> 11.5 us
  transfers between devices with their start and end apart: 4 -> 7, of which waited for: 3 -> 6; matrix products, arithmetic and copies ran while one was open for 22% -> 23% of each run, Pallas kernels for 0% -> 0%
where the time goes in v1:
time: 522 us; the launch traced here: 519 us
  matrix products  164 us (31%)
  waiting for transfers between devices  134 us (26%)
  blocking collectives  120 us (23%)
  local copies, waits for them, and re-layouts  45 us (9%)
  other arithmetic  33 us (6%)
  between operations  14 us (3%)
  starting transfers between devices  8.02 us (2%)
    pmax x1, blocking collectives, body(): row_max = lax.pmax(lax.map(local_max, (query_heads, key_heads)), 'pts')  61.1 us
    unnamed x4, waiting for transfers between devices  59 us
    psum x1, blocking collectives, body(): numer_all, total_all = lax.psum((numerator, total_cols), 'pts')  58.7 us
    dot_general x36, matrix products, masked_scores(): jnp.dot(query_head, key_head.T, preferred_element_type=jnp.float32) * 0.125  51.6 us
    ppermute x4, waiting for transfers between devices, grow_blocks(): theirs = lax.ppermute(tiles, axis, [(i, i ^ stride) for i in range(peers)])  40.6 us
    psum x1, waiting for transfers between devices, body(): numer_all, total_all = lax.psum((numerator, total_cols), 'pts')  34 us
    dot_general x12, matrix products, backward_head(): jnp.dot(grad_scores, key_head, preferred_element_type=jnp.float32) * 0.125  23.7 us
    lt x36, other arithmetic, body(): live_mask = jnp.arange(slots, dtype=jnp.int32) < counts[0]  23.4 us
  transfers between devices with their start and end apart: 7, of which 6 were waited for; matrix products, arithmetic and copies ran while one was open for 23% of the time, Pallas kernels for 0%

profile of v1, /device:TPU:0, one launch (start us, length us, event | category | flops | bytes accessed | tf_op | source)
XLA Modules:
  0.0 519.0 jit_solution(13181352839999559824)
XLA Ops:
  10.5 2.9 collective-permute-start.1
  13.4 5.2 %collective-permute-done.1 = bf16[2,64,768]{2,1,0:T(8,128)(2,1)S(1)} collective-permute-done((bf16[2,64,768]{2,1,0:T(8,128)(2,1)S(1)}, bf16[2,64,768]{2,1,0:T(8,128)(2,1)S(1)}, u32[]{:S(2)}, u32[]{:S(2)}) %collective-permute-start.1) | collective-permute-done | bytes 196640 | tf_op jit(solution)/shard_map/ppermute | solution.py:19
  20.6 8.8 %collective-permute-done.2 = bf16[4,64,768]{2,1,0:T(8,128)(2,1)S(1)} collective-permute-done((bf16[4,64,768]{2,1,0:T(8,128)(2,1)S(1)}, bf16[4,64,768]{2,1,0:T(8,128)(2,1)S(1)}, u32[]{:S(2)}, u32[]{:S(2)}) %collective-permute-start.2) | collective-permute-done | bytes 393248 | tf_op jit(solution)/shard_map/ppermute | solution.py:19
  29.6 2.6 collective-permute-start.3
  37.6 2.9 convolution_convert_fusion
  43.3 25.6 %collective-permute-done.3 = bf16[8,64,768]{2,1,0:T(8,128)(2,1)} collective-permute-done((bf16[8,64,768]{2,1,0:T(8,128)(2,1)S(1)}, bf16[8,64,768]{2,1,0:T(8,128)(2,1)}, u32[]{:S(2)}, u32[]{:S(2)}) %collective-permute-start.3) | collective-permute-done | bytes 786464 | tf_op jit(solution)/shard_map/ppermute | solution.py:19
  70.3 3.8 copy.33
  74.2 4.5 reshape_reshape.3
  78.6 2.7 copy.38
  81.4 25.9 %while.39 = (s32[]{:T(128)}, f32[12,1024]{1,0:T(8,128)S(1)}, bf16[12,1024,64]{2,1,0:T(8,128)(2,1)}, bf16[12,384,64]{2,1,0:T(8,128)(2,1)}, s32[]{:T(128)}, /*index=5*/s32[]{:T(128)}, s32[]{:T(128)}) while((s32[]{:T(128)}, f32[12,1024]{1,0:T(8,128)S(1)}, bf16[12,1024,64]{2,1,0:T(8,128)(2,1)}, bf16[12,384,64]{2,1,0:T(8,128)(2,1)}, ...), condition=%wide.region_2.3_spmd.clone, body=%wide.region_0.2_spmd.clone.sunk | while | flops 51510656 | bytes 374621 | solution.py:60
  107.3 61.1 %pmax.7 = f32[12,1024]{1,0:T(8,128)S(1)} all-reduce(f32[12,1024]{1,0:T(8,128)S(1)} %get-tuple-element.132), channel_id=1, replica_groups=mesh['groups'=2,'pts'=16] {'pts'}, use_global_device_ids=true, to_apply=%region_3.4 | all-reduce | flops 12288 | bytes 98304 | tf_op jit(solution)/shard_map/pmax | solution.py:60
  168.4 2.1 broadcast.28.clone
  170.5 50.4 %while.40 = (s32[]{:T(128)}, f32[12,1024]{1,0:T(8,128)S(1)}, f32[12,1024,64]{1,2,0:T(8,128)}, bf16[12,1024,64]{2,1,0:T(8,128)(2,1)}, bf16[12,384,64]{2,1,0:T(8,1...) while((s32[]{:T(128)}, f32[12,1024]{1,0:T(8,128)S(1)}, ...), condition=%wide.region_6.7_spmd.clone, body=%wide.region_4.6_spmd.clone.sunk | while | flops 102628736 | bytes 2321273 | solution.py:70
  220.9 3.6 copy.41
  224.6 58.7 %psum.15 = f32[1024,12]{0,1:T(8,128)S(1)} all-reduce(f32[1024,12]{0,1:T(8,128)S(1)} %bitcast.175), channel_id=1, replica_groups=mesh['groups'=2,'pts'=16] {'pts'}, use_global_device_ids=true, to_apply=%region_8.9 | all-reduce | flops 12288 | bytes 98304 | tf_op jit(solution)/shard_map/psum | solution.py:75
  285.3 3.5 copy.42
  288.9 2.7 copy.43
  291.6 34.0 %all-reduce.2.cloned.1.call-done = f32[1024,768]{1,0:T(8,128)} async-done(((f32[1024,768]{1,0:T(8,128)}), f32[1024,768]{1,0:T(8,128)}) %all-reduce.2.cloned.1.call-update) | async-done | bytes 3145744 | tf_op jit(solution)/shard_map/psum | solution.py:75
  325.6 5.6 %convert_multiply_fusion = (f32[1024,768]{1,0:T(8,128)}, bf16[1024,768]{1,0:T(8,128)(2,1)}) fusion(bf16[1024,768]{1,0:T(8,128)(2,1)S(1)} %copy-done.1, f32[1024,768]{1,0:T(8,128)} %all-reduce.2.cloned.1.call-done, f32[1024,768]{1,0:T(8,128)} %copy.42), kind=kLoop, calls=%fused_computation.57 | loop fusion | flops 3932160 | bytes 12582912 | tf_op jit(solution)/shard_map/mul | solution.py:83
  331.3 3.6 copy.44
  334.8 2.3 reduce_sum.18
  339.2 102.0 %while.41 = (s32[]{:T(128)}, f32[12,1024,64]{1,2,0:T(8,128)}, bf16[12,384,64]{1,2,0:T(8,128)(2,1)}, bf16[12,384,64]{1,2,0:T(8,128)(2,1)S(1)}, bf16[12,1024,64]{2...) while((s32[]{:T(128)}, f32[12,1024,64]{1,2,0:T(8,128)}, ...), condition=%wide.region_11.12_spmd.clone, body=%wide.region_10.11_spmd.clone.sunk | while | flops 254501248 | bytes 8648581 | solution.py:102
  441.2 3.5 copy.49
  451.3 59.0 %reduce-scatter.4.cloned.1.call-done = f32[64,768]{1,0:T(8,128)} async-done(((f32[1024,768]{1,0:T(8,128)}), f32[64,768]{1,0:T(8,128)}) %reduce-scatter.4.cloned.1.call-update) | async-done | bytes 196624
  (235 shorter events, 204.9 us)
Async XLA Ops:
  7.2 26.2 %copy-start = (bf16[768,768]{1,0:T(8,128)(2,1)S(1)}, bf16[768,768]{1,0:T(8,128)(2,1)}, u32[]{:S(2)}) copy-start(bf16[768,768]{1,0:T(8,128)(2,1)} %param.18) | copy-start | bytes 3538948
  7.2 281.7 %all-gather.2.cloned.1.call-start = ((), (), s32[]{:S(2)}) async-start(), calls=%async_computation.2 | async-start | bytes 1671168 | tf_op jit(solution)/shard_map/all_gather | solution.py:81
  9.0 1.5 collective-permute-start
  10.5 8.1 %collective-permute-start.1 = (bf16[2,64,768]{2,1,0:T(8,128)(2,1)S(1)}, bf16[2,64,768]{2,1,0:T(8,128)(2,1)S(1)}, u32[]{:S(2)}, u32[]{:S(2)}) collective-permute-start(bf16[2,64,768]{2,1,0:T(8,128)(2,1)S(1)} %pad_maximum_fusion.3), channel_id=1, source_target_pairs={{0,2},{1,3},{2,0},{3,1},{4,6},{5,7},{6,4},{7,5},{8,10},{9,11},{10,... | collective-permute-start | bytes 589832 | tf_op jit(solution)/shard_map/ppermute | solution.py:19
  18.7 10.7 %collective-permute-start.2 = (bf16[4,64,768]{2,1,0:T(8,128)(2,1)S(1)}, bf16[4,64,768]{2,1,0:T(8,128)(2,1)S(1)}, u32[]{:S(2)}, u32[]{:S(2)}) collective-permute-start(bf16[4,64,768]{2,1,0:T(8,128)(2,1)S(1)} %pad_maximum_fusion.2), channel_id=1, source_target_pairs={{0,4},{1,5},{2,6},{3,7},{4,0},{5,1},{6,2},{7,3},{8,12},{9,13},{10,... | collective-permute-start | bytes 1179656 | tf_op jit(solution)/shard_map/ppermute | solution.py:19
  20.6 11.6 %copy-start.3 = (bf16[768,768]{1,0:T(8,128)(2,1)S(1)}, bf16[768,768]{1,0:T(8,128)(2,1)}, u32[]{:S(2)}) copy-start(bf16[768,768]{1,0:T(8,128)(2,1)} %param.20) | copy-start | bytes 3538948
  20.6 11.6 %copy-start.6 = (bf16[64,768]{1,0:T(8,128)(2,1)S(1)}, bf16[64,768]{1,0:T(8,128)(2,1)}, u32[]{:S(2)}) copy-start(bf16[64,768]{1,0:T(8,128)(2,1)} %param.21) | copy-start | bytes 294916
  29.5 3.9 copy-start.8
  29.6 39.4 %collective-permute-start.3 = (bf16[8,64,768]{2,1,0:T(8,128)(2,1)S(1)}, bf16[8,64,768]{2,1,0:T(8,128)(2,1)}, u32[]{:S(2)}, u32[]{:S(2)}) collective-permute-start(bf16[8,64,768]{2,1,0:T(8,128)(2,1)S(1)} %pad_maximum_fusion.1), channel_id=1, source_target_pairs={{0,8},{1,9},{2,10},{3,11},{4,12},{5,13},{6,14},{7,15},{8,0},{9,1},... | collective-permute-start | bytes 2359304 | tf_op jit(solution)/shard_map/ppermute | solution.py:19
  33.3 292.3 %all-reduce.2.cloned.1.call-start = ((), (), s32[]{:S(2)}) async-start(), calls=%async_computation.1 | async-start | bytes 6291456 | tf_op jit(solution)/shard_map/psum | solution.py:75
  224.5 285.8 %reduce-scatter.4.cloned.1.call-start = ((), (), s32[]{:S(2)}) async-start(), calls=%async_computation.3 | async-start | bytes 3342336
  288.9 36.7 %copy-start.1 = (bf16[1024,768]{1,0:T(8,128)(2,1)S(1)}, bf16[1024,768]{1,0:T(8,128)(2,1)}, u32[]{:S(2)}) copy-start(bf16[1024,768]{1,0:T(8,128)(2,1)} %all-gather.2.cloned.1.call-done) | copy-start | bytes 4718596
  444.8 1.3 copy-start.4
  444.8 1.3 copy-start.7
  447.9 1.8 copy-start.5
  449.7 61.6 %copy-start.2 = (bf16[768,768]{1,0:T(8,128)(2,1)S(1)}, bf16[768,768]{1,0:T(8,128)(2,1)}, u32[]{:S(2)}) copy-start(bf16[768,768]{1,0:T(8,128)(2,1)} %param.17) | copy-start | bytes 3538948
Sparse Core Ops, SparseCore 0:
  33.4 57.2 all-gather.1
  224.6 100.9 all-reduce.1
  444.9 65.3 reduce-scatter.3
